TPU v7x, 256 devices: a whole 4x4x8 slice. The times are simulated.
256 devices in a mesh: sub: 32 (over y_lo, z, core), crow: 4 (over x), ccol: 2 (over y_hi).
Axes of the slice: x: 4, y: 4 (y_hi: 2, y_lo: 2; y = y_hi * 2 + y_lo), z: 8, core: 2. Of those that a mesh axis runs over, the one named last changes fastest.
Arguments:
- rhs: float32 [192, 48, 3, 10, 256], P('sub', ('crow', 'ccol')), may hold values from -6 to 6
- start: float32 [192, 48, 3, 10, 256], P('sub', ('crow', 'ccol')), may hold values from -1.75 to 1.75
- stiffness: float32 [192, 48, 3, 10], P('sub', ('crow', 'ccol')), may hold values from 0.1 to 1
- sub_inverse: bfloat16 [256, 1920, 1920], P(('sub', 'crow', 'ccol')), may hold values from -0.0625 to 0.0625
- basis: bfloat16 [256, 1920, 128], P(('sub', 'crow', 'ccol')), may hold values from -0.0625 to 0.0625
- coarse_inverse: bfloat16 [32, 512, 16384], P(None, ('crow', 'ccol'), 'sub'), may hold values from -0.09375 to 0.09375
- offsets: int32 [32, 8], P('sub'), may hold values from 0 to 464, as said below
Outputs:
- solution: float32 [192, 48, 3, 10, 256], P('sub', ('crow', 'ccol'))
Inputs may be any that keep to these rules, and one draw needn't show every extreme that they name: In every row g, offsets[g, 0] = 0 and the offsets rise; each count (next offset minus this one, 512 after the last) lies between 48 and 128, and every group has a subdomain with exactly 128.
All inputs are finite; a program needn't handle non-finite values.
Results may differ from a plain program's by a relative error of at most 0.0037.
Values may be sent and summed in bfloat16 or wider, within the bound.
A program may use at most 64 MiB of HBM per device.

v0:
```python
import jax
import jax.numpy as jnp
from jax import lax
from jax.sharding import PartitionSpec as P

ITERS = 2


def extended_2(block, sides, width):
    for axis, dim in sides:
        count = lax.axis_size(axis)
        forward = [(i, i + 1) for i in range(count - 1)]
        backward = [(target, source) for source, target in forward]
        low = lax.ppermute(
            lax.slice_in_dim(block, block.shape[dim] - width, None, axis=dim), axis, forward
        )
        high = lax.ppermute(lax.slice_in_dim(block, 0, width, axis=dim), axis, backward)
        block = jnp.concatenate([low, block, high], axis=dim)
    return block


def neighbours(widened):
    padded_z = jnp.pad(widened, ((0, 0), (0, 0), (0, 0), (1, 1), (0, 0)))
    beside = padded_z[2:, 1:-1, :, 1:-1] + padded_z[:-2, 1:-1, :, 1:-1]
    beside = beside + padded_z[1:-1, 2:, :, 1:-1] + padded_z[1:-1, :-2, :, 1:-1]
    beside = beside + padded_z[1:-1, 1:-1, :, 2:] + padded_z[1:-1, 1:-1, :, :-2]
    return beside


def shards(rhs, start, stiffness, sub_inverse, basis, coarse_inverse, offsets):
    cells_s, cells_q, comps, layers, columns = rhs.shape
    kgroup = coarse_inverse.shape[2]
    share_rows = coarse_inverse.shape[1]
    max_cols = basis.shape[2]
    group_offsets = offsets[0]
    groups = group_offsets.shape[0]
    counts = jnp.concatenate([group_offsets[1:], jnp.full((1,), kgroup, jnp.int32)]) - group_offsets
    member = lax.axis_index(("crow", "ccol"))
    sub_index = lax.axis_index("sub")
    member_ids = jnp.arange(groups, dtype=jnp.int32)
    picked = member_ids == member
    own_offset = jnp.sum(jnp.where(picked, group_offsets, 0))
    own_count = jnp.sum(jnp.where(picked, counts, 0))
    col_ids = jnp.arange(max_cols, dtype=jnp.int32)
    wanted = jnp.where(col_ids < own_count, own_offset + col_ids, -1)
    diagonal = (6.0 + stiffness)[..., None]
    flat_inverse = coarse_inverse.reshape(-1, kgroup)
    local_inverse = sub_inverse[0]
    local_basis = basis[0]
    solution = start
    for sweep in range(ITERS):
        widened = extended_2(solution, (("sub", 0), (("crow", "ccol"), 1)), 1)
        residual = rhs - (diagonal * solution - neighbours(widened))
        extended = extended_2(residual.astype(jnp.bfloat16), (("sub", 0), (("crow", "ccol"), 1)), 1)
        flat_res = extended.reshape(-1, columns)
        projected = lax.dot_general(
            local_basis, flat_res, (((0,), (0,)), ((), ())), preferred_element_type=jnp.float32
        )
        restricted = jnp.where(col_ids[:, None] < own_count, projected, 0.0).astype(jnp.bfloat16)
        place_piece = lax.all_gather(restricted, ("crow", "ccol"), axis=0, tiled=True)
        place_row_ids = jnp.arange(place_piece.shape[0], dtype=jnp.int32)
        owner_ids = place_row_ids // max_cols
        column = place_row_ids % max_cols
        matches = member_ids[:, None] == owner_ids[None, :]
        slot_base = jnp.sum(jnp.where(matches, group_offsets[:, None], 0), axis=0)
        slot_limit = jnp.sum(jnp.where(matches, counts[:, None], 0), axis=0)
        targets = jnp.where(column < slot_limit, slot_base + column, -1)
        place_selector = (jnp.arange(kgroup, dtype=jnp.int32)[:, None] == targets[None, :]).astype(
            jnp.bfloat16
        )
        placed_sum = jnp.dot(place_selector, place_piece, preferred_element_type=jnp.float32)
        coefficients = placed_sum.astype(jnp.bfloat16)
        partial_value = jnp.dot(flat_inverse, coefficients, preferred_element_type=jnp.float32)
        summed = lax.psum(partial_value, "sub")
        own_share = lax.dynamic_slice_in_dim(summed, sub_index * share_rows, share_rows, 0)
        amounts = own_share.astype(jnp.bfloat16)
        piece = lax.all_gather(amounts, ("crow", "ccol"), axis=0, tiled=True)
        row_ids = jnp.arange(piece.shape[0], dtype=jnp.int32)
        slot_ids = row_ids % share_rows * groups + row_ids // share_rows
        selector = (wanted[:, None] == slot_ids[None, :]).astype(jnp.bfloat16)
        chosen = jnp.dot(selector, piece, preferred_element_type=jnp.float32)
        chosen = chosen.astype(jnp.bfloat16)
        fine_part = jnp.dot(local_inverse, flat_res, preferred_element_type=jnp.float32)
        coarse_part = jnp.dot(local_basis, chosen, preferred_element_type=jnp.float32)
        correction = (fine_part + coarse_part).reshape(
            cells_s + 2, cells_q + 2, comps, layers, columns
        )
        solution = solution + correction[1:-1, 1:-1]
    return solution


def solution(mesh):
    return jax.shard_map(
        shards,
        mesh=mesh,
        in_specs=(
            P("sub", ("crow", "ccol"), None, None, None),
            P("sub", ("crow", "ccol"), None, None, None),
            P("sub", ("crow", "ccol"), None, None),
            P(("sub", "crow", "ccol"), None, None),
            P(("sub", "crow", "ccol"), None, None),
            P(None, ("crow", "ccol"), "sub"),
            P("sub", None),
        ),
        out_specs=P("sub", ("crow", "ccol"), None, None, None),
        check_vma=False,
    )
```

profile of v0, /device:TPU:8, one launch (start us, length us, event | category | flops | bytes accessed | tf_op | source)
XLA Modules:
  0.0 569.7 jit_solution(5922498140937865681)
XLA Ops:
  0.0 1.8 copy.60
  1.8 1.2 copy-done.2
  3.1 1.9 collective-permute-start.1
  5.1 7.1 %collective-permute-start = (f32[1,6,3,10,256]{4,3,2,1,0:T(8,128)S(1)}, f32[1,6,3,10,256]{4,3,2,1,0:T(8,128)S(1)}, u32[]{:S(2)}, u32[]{:S(2)}) collective-permute-start(f32[1,6,3,10,256]{4,3,2,1,0:T(8,128)S(1)} %get-tuple-element.15), channel_id=1, source_target_pairs={{8,0},{16,8},{24,16},{32,24},{40,32},{48,40},{56,48},{64,56},{72,6... | collective-permute-start | bytes 552968 | tf_op jit(solution)/shard_map/ppermute | solution.py:17
  13.1 1.6 collective-permute-done.1
  14.6 1.7 copy_dynamic-update-slice_fusion
  16.5 1.3 collective-permute-start.2
  17.8 6.1 %collective-permute-start.3 = (f32[8,1,3,10,256]{4,3,2,1,0:T(8,128)S(1)}, f32[8,1,3,10,256]{4,3,2,1,0:T(8,128)S(1)}, u32[]{:S(2)}, u32[]{:S(2)}) collective-permute-start(f32[8,1,3,10,256]{4,3,2,1,0:T(8,128)S(1)} %get-tuple-element.11), channel_id=1, source_target_pairs={{0,1},{1,2},{2,3},{3,4},{4,5},{5,6},{6,7},{8,9},{9,10},{10,11},{11... | collective-permute-start | bytes 737288 | tf_op jit(solution)/shard_map/ppermute | solution.py:14
  23.9 5.7 %collective-permute-done.2 = f32[8,1,3,10,256]{4,3,2,1,0:T(8,128)S(1)} collective-permute-done((f32[8,1,3,10,256]{4,3,2,1,0:T(8,128)S(1)}, f32[8,1,3,10,256]{4,3,2,1,0:T(8,128)S(1)}, u32[]{:S(2)}, u32[]{:S(2)}) %collective-permute-start.2) | collective-permute-done | bytes 245792 | tf_op jit(solution)/shard_map/ppermute | solution.py:17
  29.6 7.6 %collective-permute-done.3 = f32[8,1,3,10,256]{4,3,2,1,0:T(8,128)S(1)} collective-permute-done((f32[8,1,3,10,256]{4,3,2,1,0:T(8,128)S(1)}, f32[8,1,3,10,256]{4,3,2,1,0:T(8,128)S(1)}, u32[]{:S(2)}, u32[]{:S(2)}) %collective-permute-start.3) | collective-permute-done | bytes 245792 | tf_op jit(solution)/shard_map/ppermute | solution.py:14
  37.9 2.3 fusion.19
  40.2 1.9 collective-permute-start.4
  42.1 7.1 %collective-permute-start.5 = (bf16[1,6,3,10,256]{4,3,2,1,0:T(8,128)(2,1)S(1)}, bf16[1,6,3,10,256]{4,3,2,1,0:T(8,128)(2,1)S(1)}, u32[]{:S(2)}, u32[]{:S(2)}) collective-permute-start(bf16[1,6,3,10,256]{4,3,2,1,0:T(8,128)(2,1)S(1)} %get-tuple-element.24), channel_id=1, source_target_pairs={{8,0},{16,8},{24,16},{32,24},{40,32},{48,40},{56,48},{64,56},{72,6... | collective-permute-start | bytes 276488 | tf_op jit(solution)/shard_map/ppermute | solution.py:17
  49.3 1.2 iota_compare_fusion.14
  50.4 1.5 collective-permute-done.5
  51.9 0.8 pad_maximum_fusion.22
  52.7 5.1 collective-permute-start.6
  57.9 1.3 collective-permute-start.7
  59.2 1.8 add_select_fusion.4
  60.9 2.6 collective-permute-done.6
  63.5 3.8 collective-permute-done.7
  67.2 2.4 pad_maximum_fusion.12
  69.7 3.2 reshape.98
  72.9 1.7 fusion.34
  74.6 31.4 %all_gather.12 = bf16[1024,256]{0,1:T(8,128)(2,1)S(1)} all-gather(bf16[128,256]{0,1:T(8,128)(2,1)S(1)} %fusion.34), channel_id=1, replica_groups=mesh['sub'=32,'crow'=4,'ccol'=2] {'crow','ccol'}, dimensions={0}, use_global_device_ids=true | all-gather | bytes 589824 | tf_op jit(solution)/shard_map/all_gather | solution.py:60
  106.0 2.9 convolution_bitcast_fusion.1
  108.9 128.1 %all-reduce.4 = bf16[2048,256]{1,0:T(8,128)(2,1)} all-reduce(f32[2048,256]{1,0:T(8,128)} %convolution_bitcast_fusion.1), channel_id=1, replica_groups=mesh['sub'=32,'crow'=4,'ccol'=2] {'sub'}, use_global_device_ids=true, to_apply=%region_4.5 | all-reduce | flops 524288 | bytes 3145728 | tf_op jit(solution)/shard_map/psum | solution.py:74
  237.1 0.8 dynamic-slice_convert_fusion.1
  237.8 34.5 %all_gather.13 = bf16[512,256]{1,0:T(8,128)(2,1)S(1)} all-gather(bf16[64,256]{1,0:T(8,128)(2,1)S(1)} %dynamic-slice_convert_fusion.1), channel_id=1, replica_groups=mesh['sub'=32,'crow'=4,'ccol'=2] {'crow','ccol'}, dimensions={0}, use_global_device_ids=true | all-gather | bytes 294912 | tf_op jit(solution)/shard_map/all_gather | solution.py:77
  272.3 2.0 fusion.35
  274.3 7.6 %fusion.8 = f32[1920,256]{0,1:T(8,128)} fusion(f32[256,1920]{1,0:T(8,128)} %fusion.35, bf16[1920,256]{1,0:T(8,128)(2,1)} %reshape.98, bf16[1,1920,1920]{2,1,0:T(8,128)(2,1)} %param.10), kind=kOutput, calls=%fused_computation.16 | convolution fusion | flops 1887928320 | bytes 12288000 | tf_op jit(solution)/shard_map/dot_general | solution.py:83
  281.9 2.9 copy.59
  284.8 3.4 reshape.100
  288.2 2.4 slice_add_fusion.3
  290.6 1.9 collective-permute-start.8
  292.5 2.4 collective-permute-start.9
  294.9 2.7 collective-permute-done.8
  297.7 7.5 %collective-permute-done.9 = f32[1,6,3,10,256]{4,3,2,1,0:T(8,128)S(1)} collective-permute-done((f32[1,6,3,10,256]{4,3,2,1,0:T(8,128)S(1)}, f32[1,6,3,10,256]{4,3,2,1,0:T(8,128)S(1)}, u32[]{:S(2)}, u32[]{:S(2)}) %collective-permute-start.9) | collective-permute-done | bytes 184352 | tf_op jit(solution)/shard_map/ppermute | solution.py:14
  305.2 1.3 collective-permute-start.10
  306.5 6.2 %collective-permute-start.11 = (f32[8,1,3,10,256]{4,3,2,1,0:T(8,128)S(1)}, f32[8,1,3,10,256]{4,3,2,1,0:T(8,128)S(1)}, u32[]{:S(2)}, u32[]{:S(2)}) collective-permute-start(f32[8,1,3,10,256]{4,3,2,1,0:T(8,128)S(1)} %get-tuple-element.9), channel_id=1, source_target_pairs={{0,1},{1,2},{2,3},{3,4},{4,5},{5,6},{6,7},{8,9},{9,10},{10,11},{11... | collective-permute-start | bytes 737288 | tf_op jit(solution)/shard_map/ppermute | solution.py:14
  312.7 3.6 collective-permute-done.10
  316.4 2.2 collective-permute-done.11
  319.4 1.3 fusion.20
  320.7 1.9 collective-permute-start.12
  322.7 5.8 %collective-permute-start.13 = (bf16[1,6,3,10,256]{4,3,2,1,0:T(8,128)(2,1)S(1)}, bf16[1,6,3,10,256]{4,3,2,1,0:T(8,128)(2,1)S(1)}, u32[]{:S(2)}, u32[]{:S(2)}) collective-permute-start(bf16[1,6,3,10,256]{4,3,2,1,0:T(8,128)(2,1)S(1)} %get-tuple-element.22), channel_id=1, source_target_pairs={{8,0},{16,8},{24,16},{32,24},{40,32},{48,40},{56,48},{64,56},{72,6... | collective-permute-start | bytes 276488 | tf_op jit(solution)/shard_map/ppermute | solution.py:17
  328.4 0.9 collective-permute-done.12
  329.3 1.8 collective-permute-done.13
  331.1 5.9 %collective-permute-start.14 = (bf16[8,1,3,10,256]{4,3,2,1,0:T(8,128)(2,1)S(1)}, bf16[8,1,3,10,256]{4,3,2,1,0:T(8,128)(2,1)S(1)}, u32[]{:S(2)}, u32[]{:S(2)}) collective-permute-start(bf16[8,1,3,10,256]{4,3,2,1,0:T(8,128)(2,1)S(1)} %get-tuple-element.17), channel_id=1, source_target_pairs={{0,1},{1,2},{2,3},{3,4},{4,5},{5,6},{6,7},{8,9},{9,10},{10,11},{11... | collective-permute-start | bytes 368648 | tf_op jit(solution)/shard_map/ppermute | solution.py:14
  337.0 1.3 collective-permute-start.15
  338.3 2.6 collective-permute-done.14
  341.0 5.1 collective-permute-done.15
  346.1 1.5 pad_maximum_fusion.13
  347.6 3.2 reshape.101
  350.8 1.7 fusion.33
  352.4 31.3 %all_gather.14 = bf16[1024,256]{0,1:T(8,128)(2,1)S(1)} all-gather(bf16[128,256]{0,1:T(8,128)(2,1)S(1)} %fusion.33), channel_id=1, replica_groups=mesh['sub'=32,'crow'=4,'ccol'=2] {'crow','ccol'}, dimensions={0}, use_global_device_ids=true | all-gather | bytes 589824 | tf_op jit(solution)/shard_map/all_gather | solution.py:60
  383.8 2.9 convolution_bitcast_fusion
  386.7 127.4 %all-reduce.5 = bf16[2048,256]{1,0:T(8,128)(2,1)} all-reduce(f32[2048,256]{1,0:T(8,128)} %convolution_bitcast_fusion), channel_id=1, replica_groups=mesh['sub'=32,'crow'=4,'ccol'=2] {'sub'}, use_global_device_ids=true, to_apply=%region_5.6 | all-reduce | flops 524288 | bytes 3145728 | tf_op jit(solution)/shard_map/psum | solution.py:74
  514.9 34.5 %all_gather.15 = bf16[512,256]{1,0:T(8,128)(2,1)S(1)} all-gather(bf16[64,256]{1,0:T(8,128)(2,1)S(1)} %dynamic-slice_convert_fusion), channel_id=1, replica_groups=mesh['sub'=32,'crow'=4,'ccol'=2] {'crow','ccol'}, dimensions={0}, use_global_device_ids=true | all-gather | bytes 294912 | tf_op jit(solution)/shard_map/all_gather | solution.py:77
  549.4 2.0 fusion.36
  551.4 7.6 %fusion.14 = f32[1920,256]{0,1:T(8,128)} fusion(f32[256,1920]{1,0:T(8,128)} %fusion.36, bf16[1920,256]{1,0:T(8,128)(2,1)} %reshape.101, bf16[1,1920,1920]{2,1,0:T(8,128)(2,1)} %param.10), kind=kOutput, calls=%fused_computation.18 | convolution fusion | flops 1887928320 | bytes 12288000 | tf_op jit(solution)/shard_map/dot_general | solution.py:83
  559.0 2.9 copy.63
  561.8 3.4 reshape.102
  565.2 2.4 slice_add_fusion
  567.6 2.0 copy.64
  (44 shorter events, 3.5 us)
Async XLA Ops:
  0.0 106.0 %copy-start = (bf16[32,64,512]{2,1,0:T(8,128)(2,1)S(1)}, bf16[32,64,512]{2,1,0:T(8,128)(2,1)}, u32[]{:S(2)}) copy-start(bf16[32,64,512]{2,1,0:T(8,128)(2,1)} %param.12) | copy-start | bytes 6291460
  0.0 12.2 %copy-start.11 = (s32[1,8]{1,0:T(1,128)S(1)}, s32[1,8]{1,0:T(1,128)}, u32[]{:S(2)}) copy-start(s32[1,8]{1,0:T(1,128)} %param.13) | copy-start | bytes 100
  1.8 1.2 copy-start.2
  3.1 11.5 %collective-permute-start.1 = (f32[1,6,3,10,256]{4,3,2,1,0:T(8,128)S(1)}, f32[1,6,3,10,256]{4,3,2,1,0:T(8,128)S(1)}, u32[]{:S(2)}, u32[]{:S(2)}) collective-permute-start(f32[1,6,3,10,256]{4,3,2,1,0:T(8,128)S(1)} %get-tuple-element.16), channel_id=1, source_target_pairs={{0,8},{8,16},{16,24},{24,32},{32,40},{40,48},{48,56},{56,64},{64,7... | collective-permute-start | bytes 552968 | tf_op jit(solution)/shard_map/ppermute | solution.py:14
  5.1 11.3 %collective-permute-start = (f32[1,6,3,10,256]{4,3,2,1,0:T(8,128)S(1)}, f32[1,6,3,10,256]{4,3,2,1,0:T(8,128)S(1)}, u32[]{:S(2)}, u32[]{:S(2)}) collective-permute-start(f32[1,6,3,10,256]{4,3,2,1,0:T(8,128)S(1)} %get-tuple-element.15), channel_id=1, source_target_pairs={{8,0},{16,8},{24,16},{32,24},{40,32},{48,40},{56,48},{64,56},{72,6... | collective-permute-start | bytes 552968 | tf_op jit(solution)/shard_map/ppermute | solution.py:17
  16.3 7.5 %copy-start.8 = (f32[6,6,3,10]{3,2,1,0:T(4,128)S(1)}, f32[6,6,3,10]{3,2,1,0:T(4,128)}, u32[]{:S(2)}) copy-start(f32[6,6,3,10]{3,2,1,0:T(4,128)} %param.9) | copy-start | bytes 12964
  16.4 20.9 %copy-start.7 = (f32[1,6,3,10,256]{4,3,2,1,0:T(8,128)}, f32[1,6,3,10,256]{4,3,2,1,0:T(8,128)S(1)}, u32[]{:S(2)}) copy-start(f32[1,6,3,10,256]{4,3,2,1,0:T(8,128)S(1)} %collective-permute-done) | copy-start | bytes 552964
  16.5 13.2 %collective-permute-start.2 = (f32[8,1,3,10,256]{4,3,2,1,0:T(8,128)S(1)}, f32[8,1,3,10,256]{4,3,2,1,0:T(8,128)S(1)}, u32[]{:S(2)}, u32[]{:S(2)}) collective-permute-start(f32[8,1,3,10,256]{4,3,2,1,0:T(8,128)S(1)} %get-tuple-element.12), channel_id=1, source_target_pairs={{1,0},{2,1},{3,2},{4,3},{5,4},{6,5},{7,6},{9,8},{10,9},{11,10},{12... | collective-permute-start | bytes 737288 | tf_op jit(solution)/shard_map/ppermute | solution.py:17
  17.8 19.5 %collective-permute-start.3 = (f32[8,1,3,10,256]{4,3,2,1,0:T(8,128)S(1)}, f32[8,1,3,10,256]{4,3,2,1,0:T(8,128)S(1)}, u32[]{:S(2)}, u32[]{:S(2)}) collective-permute-start(f32[8,1,3,10,256]{4,3,2,1,0:T(8,128)S(1)} %get-tuple-element.11), channel_id=1, source_target_pairs={{0,1},{1,2},{2,3},{3,4},{4,5},{5,6},{6,7},{8,9},{9,10},{10,11},{11... | collective-permute-start | bytes 737288 | tf_op jit(solution)/shard_map/ppermute | solution.py:14
  23.9 14.0 %copy-start.3 = (f32[6,6,3,10,256]{4,3,2,1,0:T(8,128)S(1)}, f32[6,6,3,10,256]{4,3,2,1,0:T(8,128)}, u32[]{:S(2)}) copy-start(f32[6,6,3,10,256]{4,3,2,1,0:T(8,128)} %copy-done.2) | copy-start | bytes 3317764
  23.9 14.0 %copy-start.5 = (f32[6,6,3,10,256]{4,2,3,1,0:T(4,128)S(1)}, f32[6,6,3,10,256]{4,2,3,1,0:T(4,128)}, u32[]{:S(2)}) copy-start(f32[6,6,3,10,256]{4,2,3,1,0:T(4,128)} %param.7) | copy-start | bytes 3317764
  40.2 10.2 %collective-permute-start.4 = (bf16[1,6,3,10,256]{4,3,2,1,0:T(8,128)(2,1)S(1)}, bf16[1,6,3,10,256]{4,3,2,1,0:T(8,128)(2,1)S(1)}, u32[]{:S(2)}, u32[]{:S(2)}) collective-permute-start(bf16[1,6,3,10,256]{4,3,2,1,0:T(8,128)(2,1)S(1)} %get-tuple-element.23), channel_id=1, source_target_pairs={{0,8},{8,16},{16,24},{24,32},{32,40},{40,48},{48,56},{56,64},{64,7... | collective-permute-start | bytes 276488 | tf_op jit(solution)/shard_map/ppermute | solution.py:14
  42.1 9.8 %collective-permute-start.5 = (bf16[1,6,3,10,256]{4,3,2,1,0:T(8,128)(2,1)S(1)}, bf16[1,6,3,10,256]{4,3,2,1,0:T(8,128)(2,1)S(1)}, u32[]{:S(2)}, u32[]{:S(2)}) collective-permute-start(bf16[1,6,3,10,256]{4,3,2,1,0:T(8,128)(2,1)S(1)} %get-tuple-element.24), channel_id=1, source_target_pairs={{8,0},{16,8},{24,16},{32,24},{40,32},{48,40},{56,48},{64,56},{72,6... | collective-permute-start | bytes 276488 | tf_op jit(solution)/shard_map/ppermute | solution.py:17
  52.7 10.8 %collective-permute-start.6 = (bf16[8,1,3,10,256]{4,3,2,1,0:T(8,128)(2,1)}, bf16[8,1,3,10,256]{4,3,2,1,0:T(8,128)(2,1)S(1)}, u32[]{:S(2)}, u32[]{:S(2)}) collective-permute-start(bf16[8,1,3,10,256]{4,3,2,1,0:T(8,128)(2,1)} %get-tuple-element.19), channel_id=1, source_target_pairs={{0,1},{1,2},{2,3},{3,4},{4,5},{5,6},{6,7},{8,9},{9,10},{10,11},{11... | collective-permute-start | bytes 368648 | tf_op jit(solution)/shard_map/ppermute | solution.py:14
  57.9 9.4 %collective-permute-start.7 = (bf16[8,1,3,10,256]{4,3,2,1,0:T(8,128)(2,1)}, bf16[8,1,3,10,256]{4,3,2,1,0:T(8,128)(2,1)}, u32[]{:S(2)}, u32[]{:S(2)}) collective-permute-start(bf16[8,1,3,10,256]{4,3,2,1,0:T(8,128)(2,1)} %get-tuple-element.20), channel_id=1, source_target_pairs={{1,0},{2,1},{3,2},{4,3},{5,4},{6,5},{7,6},{9,8},{10,9},{11,10},{12... | collective-permute-start | bytes 368648 | tf_op jit(solution)/shard_map/ppermute | solution.py:17
  69.7 3.2 copy-start.4
  69.7 3.2 copy-start.9
  108.9 163.4 %copy-start.10 = (s32[128]{0:T(128)S(1)}, s32[128]{0:T(128)}, u32[]{:S(2)}) copy-start(s32[128]{0:T(128)} %add_select_fusion.4) | copy-start | bytes 1540
  290.5 28.8 %copy-start.1 = (f32[6,6,3,10,256]{4,3,2,1,0:T(8,128)}, f32[6,6,3,10,256]{4,3,2,1,0:T(8,128)S(1)}, u32[]{:S(2)}) copy-start(f32[6,6,3,10,256]{4,3,2,1,0:T(8,128)S(1)} %slice_add_fusion.3) | copy-start | bytes 3317764
  290.6 7.1 %collective-permute-start.8 = (f32[1,6,3,10,256]{4,3,2,1,0:T(8,128)S(1)}, f32[1,6,3,10,256]{4,3,2,1,0:T(8,128)S(1)}, u32[]{:S(2)}, u32[]{:S(2)}) collective-permute-start(f32[1,6,3,10,256]{4,3,2,1,0:T(8,128)S(1)} %get-tuple-element.14), channel_id=1, source_target_pairs={{8,0},{16,8},{24,16},{32,24},{40,32},{48,40},{56,48},{64,56},{72,6... | collective-permute-start | bytes 552968 | tf_op jit(solution)/shard_map/ppermute | solution.py:17
  292.5 12.6 %collective-permute-start.9 = (f32[1,6,3,10,256]{4,3,2,1,0:T(8,128)S(1)}, f32[1,6,3,10,256]{4,3,2,1,0:T(8,128)S(1)}, u32[]{:S(2)}, u32[]{:S(2)}) collective-permute-start(f32[1,6,3,10,256]{4,3,2,1,0:T(8,128)S(1)} %get-tuple-element.13), channel_id=1, source_target_pairs={{0,8},{8,16},{16,24},{24,32},{32,40},{40,48},{48,56},{56,64},{64,7... | collective-permute-start | bytes 552968 | tf_op jit(solution)/shard_map/ppermute | solution.py:14
  305.2 11.2 %collective-permute-start.10 = (f32[8,1,3,10,256]{4,3,2,1,0:T(8,128)S(1)}, f32[8,1,3,10,256]{4,3,2,1,0:T(8,128)S(1)}, u32[]{:S(2)}, u32[]{:S(2)}) collective-permute-start(f32[8,1,3,10,256]{4,3,2,1,0:T(8,128)S(1)} %get-tuple-element.10), channel_id=1, source_target_pairs={{1,0},{2,1},{3,2},{4,3},{5,4},{6,5},{7,6},{9,8},{10,9},{11,10},{12... | collective-permute-start | bytes 737288 | tf_op jit(solution)/shard_map/ppermute | solution.py:17
  306.5 12.9 %copy-start.6 = (f32[6,6,3,10,256]{4,2,3,1,0:T(4,128)S(1)}, f32[6,6,3,10,256]{4,2,3,1,0:T(4,128)}, u32[]{:S(2)}) copy-start(f32[6,6,3,10,256]{4,2,3,1,0:T(4,128)} %param.7) | copy-start | bytes 3317764
  306.5 12.1 %collective-permute-start.11 = (f32[8,1,3,10,256]{4,3,2,1,0:T(8,128)S(1)}, f32[8,1,3,10,256]{4,3,2,1,0:T(8,128)S(1)}, u32[]{:S(2)}, u32[]{:S(2)}) collective-permute-start(f32[8,1,3,10,256]{4,3,2,1,0:T(8,128)S(1)} %get-tuple-element.9), channel_id=1, source_target_pairs={{0,1},{1,2},{2,3},{3,4},{4,5},{5,6},{6,7},{8,9},{9,10},{10,11},{11... | collective-permute-start | bytes 737288 | tf_op jit(solution)/shard_map/ppermute | solution.py:14
  320.7 8.6 %collective-permute-start.12 = (bf16[1,6,3,10,256]{4,3,2,1,0:T(8,128)(2,1)S(1)}, bf16[1,6,3,10,256]{4,3,2,1,0:T(8,128)(2,1)S(1)}, u32[]{:S(2)}, u32[]{:S(2)}) collective-permute-start(bf16[1,6,3,10,256]{4,3,2,1,0:T(8,128)(2,1)S(1)} %get-tuple-element.21), channel_id=1, source_target_pairs={{0,8},{8,16},{16,24},{24,32},{32,40},{40,48},{48,56},{56,64},{64,7... | collective-permute-start | bytes 276488 | tf_op jit(solution)/shard_map/ppermute | solution.py:14
  322.7 8.4 %collective-permute-start.13 = (bf16[1,6,3,10,256]{4,3,2,1,0:T(8,128)(2,1)S(1)}, bf16[1,6,3,10,256]{4,3,2,1,0:T(8,128)(2,1)S(1)}, u32[]{:S(2)}, u32[]{:S(2)}) collective-permute-start(bf16[1,6,3,10,256]{4,3,2,1,0:T(8,128)(2,1)S(1)} %get-tuple-element.22), channel_id=1, source_target_pairs={{8,0},{16,8},{24,16},{32,24},{40,32},{48,40},{56,48},{64,56},{72,6... | collective-permute-start | bytes 276488 | tf_op jit(solution)/shard_map/ppermute | solution.py:17
  331.1 9.8 %collective-permute-start.14 = (bf16[8,1,3,10,256]{4,3,2,1,0:T(8,128)(2,1)S(1)}, bf16[8,1,3,10,256]{4,3,2,1,0:T(8,128)(2,1)S(1)}, u32[]{:S(2)}, u32[]{:S(2)}) collective-permute-start(bf16[8,1,3,10,256]{4,3,2,1,0:T(8,128)(2,1)S(1)} %get-tuple-element.17), channel_id=1, source_target_pairs={{0,1},{1,2},{2,3},{3,4},{4,5},{5,6},{6,7},{8,9},{9,10},{10,11},{11... | collective-permute-start | bytes 368648 | tf_op jit(solution)/shard_map/ppermute | solution.py:14
  337.0 9.1 %collective-permute-start.15 = (bf16[8,1,3,10,256]{4,3,2,1,0:T(8,128)(2,1)S(1)}, bf16[8,1,3,10,256]{4,3,2,1,0:T(8,128)(2,1)S(1)}, u32[]{:S(2)}, u32[]{:S(2)}) collective-permute-start(bf16[8,1,3,10,256]{4,3,2,1,0:T(8,128)(2,1)S(1)} %get-tuple-element.18), channel_id=1, source_target_pairs={{1,0},{2,1},{3,2},{4,3},{5,4},{6,5},{7,6},{9,8},{10,9},{11,10},{12... | collective-permute-start | bytes 368648 | tf_op jit(solution)/shard_map/ppermute | solution.py:17
where the time goes:
time: 571 us; the launch traced here: 570 us
  blocking collectives  387 us (68%)
  starting transfers between devices  58.5 us (10%)
  waiting for transfers between devices  49.3 us (9%)
  matrix products  28.4 us (5%)
  local copies, waits for them, and re-layouts  27.4 us (5%)
  other arithmetic  18.3 us (3%)
    psum x2, blocking collectives, shards(): summed = lax.psum(partial_value, 'sub')  256 us
    all_gather x2, blocking collectives, shards(): piece = lax.all_gather(amounts, ('crow', 'ccol'), axis=0, tiled=True)  69 us
    all_gather x2, blocking collectives, shards(): lax.all_gather(restricted, ('crow', 'ccol'), axis=0, tiled=True)  62.8 us
    ppermute x8, starting transfers between devices, extended_2(): lax.ppermute(lax.slice_in_dim(block, block.shape[dim] - width, None, axis...  31.5 us
    ppermute x8, starting transfers between devices, extended_2(): lax.ppermute(lax.slice_in_dim(block, 0, width, axis=dim), axis, backward)  27 us
    ppermute x8, waiting for transfers between devices, extended_2(): lax.ppermute(lax.slice_in_dim(block, block.shape[dim] - width, None, axis...  25 us
    ppermute x8, waiting for transfers between devices, extended_2(): lax.ppermute(lax.slice_in_dim(block, 0, width, axis=dim), axis, backward)  24.3 us
    dot_general x2, matrix products, shards(): jnp.dot(local_inverse, flat_res, preferred_element_type=jnp.float32)  15.2 us
  transfers between devices with their start and end apart: 16, of which 14 were waited for; matrix products, arithmetic and copies ran while one was open for 1% of the time, Pallas kernels for 0%

commit v1 on v0

--- a/solution.py
+++ b/solution.py
@@ -57,7 +57,12 @@
             local_basis, flat_res, (((0,), (0,)), ((), ())), preferred_element_type=jnp.float32
         )
         restricted = jnp.where(col_ids[:, None] < own_count, projected, 0.0).astype(jnp.bfloat16)
-        place_piece = lax.all_gather(restricted, ("crow", "ccol"), axis=0, tiled=True)
+        place_piece = jnp.concatenate(
+            lax.all_to_all(
+                jnp.stack([restricted] * lax.axis_size(("crow", "ccol"))), ("crow", "ccol"), 0, 0
+            ),
+            axis=0,
+        )
         place_row_ids = jnp.arange(place_piece.shape[0], dtype=jnp.int32)
         owner_ids = place_row_ids // max_cols
         column = place_row_ids % max_cols

time: 571 us -> 546 us (0.956)
  blocking collectives: 387 us -> 345 us
  waiting for transfers between devices: 49.3 us -> 60.4 us
  starting transfers between devices: 58.5 us -> 64.5 us
    all_gather x2 -> x0, blocking collectives: 62.8 us -> none  [shards(): lax.all_gather(restricted, ('crow', 'ccol'), axis=0, tiled=True)]
    all_to_all x0 -> x1, blocking collectives: none -> 15.1 us  [shards(): lax.all_to_all(jnp.stack([restricted] * lax.axis_size(('crow', 'ccol'))),...]
    all_to_all x0 -> x1, waiting for transfers between devices: none -> 8.3 us  [shards(): lax.all_to_all(jnp.stack([restricted] * lax.axis_size(('crow', 'ccol'))),...]
    all_to_all x0 -> x1, starting transfers between devices: none -> 6.03 us  [shards(): lax.all_to_all(jnp.stack([restricted] * lax.axis_size(('crow', 'ccol'))),...]
  transfers between devices with their start and end apart: 16 -> 17, of which waited for: 14 -> 17; matrix products, arithmetic and copies ran while one was open for 1% -> 1% of each run, Pallas kernels for 0% -> 0%
where the time goes in v1:
time: 546 us; the launch traced here: 545 us
  blocking collectives  345 us (63%)
  starting transfers between devices  64.5 us (12%)
  waiting for transfers between devices  60.4 us (11%)
  matrix products  28.3 us (5%)
  local copies, waits for them, and re-layouts  28.2 us (5%)
  other arithmetic  17.4 us (3%)
    psum x2, blocking collectives, shards(): summed = lax.psum(partial_value, 'sub')  261 us
    all_gather x2, blocking collectives, shards(): piece = lax.all_gather(amounts, ('crow', 'ccol'), axis=0, tiled=True)  69.1 us
    ppermute x8, starting transfers between devices, extended_2(): lax.ppermute(lax.slice_in_dim(block, block.shape[dim] - width, None, axis...  31.4 us
    ppermute x8, starting transfers between devices, extended_2(): lax.ppermute(lax.slice_in_dim(block, 0, width, axis=dim), axis, backward)  27 us
    ppermute x8, waiting for transfers between devices, extended_2(): lax.ppermute(lax.slice_in_dim(block, block.shape[dim] - width, None, axis...  26.2 us
    ppermute x8, waiting for transfers between devices, extended_2(): lax.ppermute(lax.slice_in_dim(block, 0, width, axis=dim), axis, backward)  25.9 us
    dot_general x2, matrix products, shards(): jnp.dot(local_inverse, flat_res, preferred_element_type=jnp.float32)  15.2 us
    all_to_all x1, blocking collectives, shards(): lax.all_to_all(jnp.stack([restricted] * lax.axis_size(('crow', 'ccol'))),...  15.1 us
  transfers between devices with their start and end apart: 17, of which 17 were waited for; matrix products, arithmetic and copies ran while one was open for 1% of the time, Pallas kernels for 0%

profile of v1, /device:TPU:8, one launch (start us, length us, event | category | flops | bytes accessed | tf_op | source)
XLA Modules:
  0.0 544.6 jit_solution(9620116732673233271)
XLA Ops:
  0.0 1.8 copy.69
  1.9 1.9 collective-permute-start.1
  3.8 7.1 %collective-permute-start = (f32[1,6,3,10,256]{4,3,2,1,0:T(8,128)S(1)}, f32[1,6,3,10,256]{4,3,2,1,0:T(8,128)S(1)}, u32[]{:S(2)}, u32[]{:S(2)}) collective-permute-start(f32[1,6,3,10,256]{4,3,2,1,0:T(8,128)S(1)} %get-tuple-element.15), channel_id=1, source_target_pairs={{8,0},{16,8},{24,16},{32,24},{40,32},{48,40},{56,48},{64,56},{72,6... | collective-permute-start | bytes 552968 | tf_op jit(solution)/shard_map/ppermute | solution.py:17
  10.9 2.5 collective-permute-done.1
  13.7 1.4 collective-permute-done
  15.2 1.4 copy-done.2
  16.6 0.9 fusion.74
  17.5 1.3 collective-permute-start.2
  18.8 6.1 %collective-permute-start.3 = (f32[8,1,3,10,256]{4,3,2,1,0:T(8,128)}, f32[8,1,3,10,256]{4,3,2,1,0:T(8,128)S(1)}, u32[]{:S(2)}, u32[]{:S(2)}) collective-permute-start(f32[8,1,3,10,256]{4,3,2,1,0:T(8,128)} %get-tuple-element.11), channel_id=1, source_target_pairs={{0,1},{1,2},{2,3},{3,4},{4,5},{5,6},{6,7},{8,9},{9,10},{10,11},{11... | collective-permute-start | bytes 737288 | tf_op jit(solution)/shard_map/ppermute | solution.py:14
  25.0 0.9 broadcast_add_fusion
  25.9 5.0 collective-permute-done.2
  30.9 7.7 %collective-permute-done.3 = f32[8,1,3,10,256]{4,3,2,1,0:T(8,128)S(1)} collective-permute-done((f32[8,1,3,10,256]{4,3,2,1,0:T(8,128)}, f32[8,1,3,10,256]{4,3,2,1,0:T(8,128)S(1)}, u32[]{:S(2)}, u32[]{:S(2)}) %collective-permute-start.3) | collective-permute-done | bytes 245792 | tf_op jit(solution)/shard_map/ppermute | solution.py:14
  38.6 2.2 select_maximum_fusion.4
  40.9 1.5 fusion.19
  42.5 1.9 collective-permute-start.4
  44.4 7.1 %collective-permute-start.5 = (bf16[1,6,3,10,256]{4,3,2,1,0:T(8,128)(2,1)S(1)}, bf16[1,6,3,10,256]{4,3,2,1,0:T(8,128)(2,1)S(1)}, u32[]{:S(2)}, u32[]{:S(2)}) collective-permute-start(bf16[1,6,3,10,256]{4,3,2,1,0:T(8,128)(2,1)S(1)} %get-tuple-element.24), channel_id=1, source_target_pairs={{8,0},{16,8},{24,16},{32,24},{40,32},{48,40},{56,48},{64,56},{72,6... | collective-permute-start | bytes 276488 | tf_op jit(solution)/shard_map/ppermute | solution.py:17
  52.4 1.8 collective-permute-done.5
  54.2 5.1 collective-permute-start.6
  59.3 1.3 collective-permute-start.7
  61.2 3.4 collective-permute-done.6
  64.7 3.7 collective-permute-done.7
  68.4 1.5 pad_maximum_fusion.12
  69.9 3.2 reshape.108
  73.1 1.7 fusion.34
  75.7 6.0 %all-to-all-start = ((bf16[8,128,256]{2,1,0:T(8,128)(2,1)}), bf16[8,128,256]{2,1,0:T(8,128)(2,1)S(1)}, u32[]{:S(2)}, u32[]{:S(2)}) async-start(bf16[8,128,256]{2,1,0:T(8,128)(2,1)} %stack.4), calls=%async_computation | async-start | bytes 1048576 | tf_op jit(solution)/shard_map/all_to_all | solution.py:61
  81.7 1.3 add_select_fusion.4
  83.1 8.3 %all-to-all-done = bf16[8,128,256]{2,1,0:T(8,128)(2,1)S(1)} async-done(((bf16[8,128,256]{2,1,0:T(8,128)(2,1)}), bf16[8,128,256]{2,1,0:T(8,128)(2,1)S(1)}, u32[]{:S(2)}, u32[]{:S(2)}) %all-to-all-start) | async-done | bytes 524320 | tf_op jit(solution)/shard_map/all_to_all | solution.py:61
  91.4 2.9 convolution_bitcast_fusion.1
  94.3 131.4 %all-reduce.4 = bf16[2048,256]{1,0:T(8,128)(2,1)} all-reduce(f32[2048,256]{1,0:T(8,128)} %convolution_bitcast_fusion.1), channel_id=1, replica_groups=mesh['sub'=32,'crow'=4,'ccol'=2] {'sub'}, use_global_device_ids=true, to_apply=%region_4.5 | all-reduce | flops 524288 | bytes 3145728 | tf_op jit(solution)/shard_map/psum | solution.py:79
  226.4 34.5 %all_gather.6 = bf16[512,256]{1,0:T(8,128)(2,1)S(1)} all-gather(bf16[64,256]{1,0:T(8,128)(2,1)S(1)} %dynamic-slice_convert_fusion.1), channel_id=1, replica_groups=mesh['sub'=32,'crow'=4,'ccol'=2] {'crow','ccol'}, dimensions={0}, use_global_device_ids=true | all-gather | bytes 294912 | tf_op jit(solution)/shard_map/all_gather | solution.py:82
  260.9 2.0 fusion.35
  262.9 7.6 %fusion.8 = f32[1920,256]{0,1:T(8,128)} fusion(f32[256,1920]{1,0:T(8,128)} %fusion.35, bf16[1920,256]{1,0:T(8,128)(2,1)} %reshape.108, bf16[1,1920,1920]{2,1,0:T(8,128)(2,1)} %param.10), kind=kOutput, calls=%fused_computation.16 | convolution fusion | flops 1887928320 | bytes 12288000 | tf_op jit(solution)/shard_map/dot_general | solution.py:88
  270.5 2.8 copy.68
  273.4 3.4 reshape.111
  276.7 2.4 slice_add_fusion.3
  279.2 1.9 collective-permute-start.8
  281.1 2.4 collective-permute-start.9
  283.5 2.8 collective-permute-done.8
  286.3 7.3 %collective-permute-done.9 = f32[1,6,3,10,256]{4,3,2,1,0:T(8,128)S(1)} collective-permute-done((f32[1,6,3,10,256]{4,3,2,1,0:T(8,128)S(1)}, f32[1,6,3,10,256]{4,3,2,1,0:T(8,128)S(1)}, u32[]{:S(2)}, u32[]{:S(2)}) %collective-permute-start.9) | collective-permute-done | bytes 184352 | tf_op jit(solution)/shard_map/ppermute | solution.py:14
  293.8 1.3 collective-permute-start.10
  295.1 6.2 %collective-permute-start.11 = (f32[8,1,3,10,256]{4,3,2,1,0:T(8,128)S(1)}, f32[8,1,3,10,256]{4,3,2,1,0:T(8,128)S(1)}, u32[]{:S(2)}, u32[]{:S(2)}) collective-permute-start(f32[8,1,3,10,256]{4,3,2,1,0:T(8,128)S(1)} %get-tuple-element.9), channel_id=1, source_target_pairs={{0,1},{1,2},{2,3},{3,4},{4,5},{5,6},{6,7},{8,9},{9,10},{10,11},{11... | collective-permute-start | bytes 737288 | tf_op jit(solution)/shard_map/ppermute | solution.py:14
  301.3 3.6 collective-permute-done.10
  304.9 2.2 collective-permute-done.11
  308.0 1.3 fusion.20
  309.3 1.9 collective-permute-start.12
  311.2 5.8 %collective-permute-start.13 = (bf16[1,6,3,10,256]{4,3,2,1,0:T(8,128)(2,1)S(1)}, bf16[1,6,3,10,256]{4,3,2,1,0:T(8,128)(2,1)S(1)}, u32[]{:S(2)}, u32[]{:S(2)}) collective-permute-start(bf16[1,6,3,10,256]{4,3,2,1,0:T(8,128)(2,1)S(1)} %get-tuple-element.22), channel_id=1, source_target_pairs={{8,0},{16,8},{24,16},{32,24},{40,32},{48,40},{56,48},{64,56},{72,6... | collective-permute-start | bytes 276488 | tf_op jit(solution)/shard_map/ppermute | solution.py:17
  317.9 1.8 collective-permute-done.13
  319.7 5.9 %collective-permute-start.14 = (bf16[8,1,3,10,256]{4,3,2,1,0:T(8,128)(2,1)S(1)}, bf16[8,1,3,10,256]{4,3,2,1,0:T(8,128)(2,1)S(1)}, u32[]{:S(2)}, u32[]{:S(2)}) collective-permute-start(bf16[8,1,3,10,256]{4,3,2,1,0:T(8,128)(2,1)S(1)} %get-tuple-element.17), channel_id=1, source_target_pairs={{0,1},{1,2},{2,3},{3,4},{4,5},{5,6},{6,7},{8,9},{9,10},{10,11},{11... | collective-permute-start | bytes 368648 | tf_op jit(solution)/shard_map/ppermute | solution.py:14
  325.6 1.3 collective-permute-start.15
  326.9 2.0 collective-permute-done.14
  328.9 5.8 %collective-permute-done.15 = bf16[8,1,3,10,256]{4,3,2,1,0:T(8,128)(2,1)S(1)} collective-permute-done((bf16[8,1,3,10,256]{4,3,2,1,0:T(8,128)(2,1)S(1)}, bf16[8,1,3,10,256]{4,3,2,1,0:T(8,128)(2,1)S(1)}, u32[]{:S(2)}, u32[]{:S(2)}) %collective-permute-start.15) | collective-permute-done | bytes 122912 | tf_op jit(solution)/shard_map/ppermute | solution.py:17
  334.7 1.5 pad_maximum_fusion.13
  336.2 3.1 reshape.112
  339.3 1.7 fusion.33
  341.2 15.1 %all_to_all.10 = bf16[8,128,256]{2,1,0:T(8,128)(2,1)S(1)} all-to-all(bf16[8,128,256]{2,1,0:T(8,128)(2,1)S(1)} %stack.5), channel_id=1, replica_groups=mesh['sub'=32,'crow'=4,'ccol'=2] {'crow','ccol'}, dimensions={0} | all-to-all | bytes 1048576 | tf_op jit(solution)/shard_map/all_to_all | solution.py:61
  356.3 2.9 convolution_bitcast_fusion
  359.2 129.7 %all-reduce.5 = bf16[2048,256]{1,0:T(8,128)(2,1)} all-reduce(f32[2048,256]{1,0:T(8,128)} %convolution_bitcast_fusion), channel_id=1, replica_groups=mesh['sub'=32,'crow'=4,'ccol'=2] {'sub'}, use_global_device_ids=true, to_apply=%region_5.6 | all-reduce | flops 524288 | bytes 3145728 | tf_op jit(solution)/shard_map/psum | solution.py:79
  489.7 34.6 %all_gather.7 = bf16[512,256]{1,0:T(8,128)(2,1)S(1)} all-gather(bf16[64,256]{1,0:T(8,128)(2,1)S(1)} %dynamic-slice_convert_fusion), channel_id=1, replica_groups=mesh['sub'=32,'crow'=4,'ccol'=2] {'crow','ccol'}, dimensions={0}, use_global_device_ids=true | all-gather | bytes 294912 | tf_op jit(solution)/shard_map/all_gather | solution.py:82
  524.3 2.0 fusion.36
  526.3 7.6 %fusion.14 = f32[1920,256]{0,1:T(8,128)} fusion(f32[256,1920]{1,0:T(8,128)} %fusion.36, bf16[1920,256]{1,0:T(8,128)(2,1)} %reshape.112, bf16[1,1920,1920]{2,1,0:T(8,128)(2,1)} %param.10), kind=kOutput, calls=%fused_computation.18 | convolution fusion | flops 1887928320 | bytes 12288000 | tf_op jit(solution)/shard_map/dot_general | solution.py:88
  533.9 2.8 copy.73
  536.8 3.4 reshape.114
  540.1 2.4 slice_add_fusion
  542.5 2.0 copy.74
  (47 shorter events, 6.6 us)
Async XLA Ops:
  0.0 91.4 %copy-start = (bf16[32,64,512]{2,1,0:T(8,128)(2,1)S(1)}, bf16[32,64,512]{2,1,0:T(8,128)(2,1)}, u32[]{:S(2)}) copy-start(bf16[32,64,512]{2,1,0:T(8,128)(2,1)} %param.12) | copy-start | bytes 6291460
  0.0 13.4 %copy-start.4 = (f32[6,6,3,10,256]{4,2,3,1,0:T(4,128)S(1)}, f32[6,6,3,10,256]{4,2,3,1,0:T(4,128)}, u32[]{:S(2)}) copy-start(f32[6,6,3,10,256]{4,2,3,1,0:T(4,128)} %param.8) | copy-start | bytes 3317764
  1.8 9.1 %copy-start.5 = (f32[6,6,3,10,256]{4,3,2,1,0:T(8,128)}, f32[6,6,3,10,256]{4,3,2,1,0:T(8,128)S(1)}, u32[]{:S(2)}) copy-start(f32[6,6,3,10,256]{4,3,2,1,0:T(8,128)S(1)} %copy.69) | copy-start | bytes 3317764
  1.9 11.5 %collective-permute-start.1 = (f32[1,6,3,10,256]{4,3,2,1,0:T(8,128)S(1)}, f32[1,6,3,10,256]{4,3,2,1,0:T(8,128)S(1)}, u32[]{:S(2)}, u32[]{:S(2)}) collective-permute-start(f32[1,6,3,10,256]{4,3,2,1,0:T(8,128)S(1)} %get-tuple-element.16), channel_id=1, source_target_pairs={{0,8},{8,16},{16,24},{24,32},{32,40},{40,48},{48,56},{56,64},{64,7... | collective-permute-start | bytes 552968 | tf_op jit(solution)/shard_map/ppermute | solution.py:14
  3.8 11.3 %collective-permute-start = (f32[1,6,3,10,256]{4,3,2,1,0:T(8,128)S(1)}, f32[1,6,3,10,256]{4,3,2,1,0:T(8,128)S(1)}, u32[]{:S(2)}, u32[]{:S(2)}) collective-permute-start(f32[1,6,3,10,256]{4,3,2,1,0:T(8,128)S(1)} %get-tuple-element.15), channel_id=1, source_target_pairs={{8,0},{16,8},{24,16},{32,24},{40,32},{48,40},{56,48},{64,56},{72,6... | collective-permute-start | bytes 552968 | tf_op jit(solution)/shard_map/ppermute | solution.py:17
  13.7 11.2 %copy-start.10 = (s32[1,8]{1,0:T(1,128)S(1)}, s32[1,8]{1,0:T(1,128)}, u32[]{:S(2)}) copy-start(s32[1,8]{1,0:T(1,128)} %param.13) | copy-start | bytes 100
  15.2 1.4 copy-start.2
  17.5 13.4 %collective-permute-start.2 = (f32[8,1,3,10,256]{4,3,2,1,0:T(8,128)}, f32[8,1,3,10,256]{4,3,2,1,0:T(8,128)S(1)}, u32[]{:S(2)}, u32[]{:S(2)}) collective-permute-start(f32[8,1,3,10,256]{4,3,2,1,0:T(8,128)} %get-tuple-element.12), channel_id=1, source_target_pairs={{1,0},{2,1},{3,2},{4,3},{5,4},{6,5},{7,6},{9,8},{10,9},{11,10},{12... | collective-permute-start | bytes 737288 | tf_op jit(solution)/shard_map/ppermute | solution.py:17
  18.8 19.8 %collective-permute-start.3 = (f32[8,1,3,10,256]{4,3,2,1,0:T(8,128)}, f32[8,1,3,10,256]{4,3,2,1,0:T(8,128)S(1)}, u32[]{:S(2)}, u32[]{:S(2)}) collective-permute-start(f32[8,1,3,10,256]{4,3,2,1,0:T(8,128)} %get-tuple-element.11), channel_id=1, source_target_pairs={{0,1},{1,2},{2,3},{3,4},{4,5},{5,6},{6,7},{8,9},{9,10},{10,11},{11... | collective-permute-start | bytes 737288 | tf_op jit(solution)/shard_map/ppermute | solution.py:14
  25.9 15.0 %copy-start.3 = (f32[8,6,3,10,256]{4,3,2,1,0:T(8,128)S(1)}, f32[8,6,3,10,256]{4,3,2,1,0:T(8,128)}, u32[]{:S(2)}) copy-start(f32[8,6,3,10,256]{4,3,2,1,0:T(8,128)} %copy-done.2) | copy-start | bytes 4423684
  25.9 15.0 %copy-start.6 = (f32[6,6,3,10,256]{4,3,2,1,0:T(8,128)S(1)}, f32[6,6,3,10,256]{4,3,2,1,0:T(8,128)}, u32[]{:S(2)}) copy-start(f32[6,6,3,10,256]{4,3,2,1,0:T(8,128)} %copy-done.5) | copy-start | bytes 3317764
  25.9 15.0 %copy-start.8 = (f32[6,6,3,10,256]{4,2,3,1,0:T(4,128)S(1)}, f32[6,6,3,10,256]{4,2,3,1,0:T(4,128)}, u32[]{:S(2)}) copy-start(f32[6,6,3,10,256]{4,2,3,1,0:T(4,128)} %param.7) | copy-start | bytes 3317764
  42.5 9.9 %collective-permute-start.4 = (bf16[1,6,3,10,256]{4,3,2,1,0:T(8,128)(2,1)S(1)}, bf16[1,6,3,10,256]{4,3,2,1,0:T(8,128)(2,1)S(1)}, u32[]{:S(2)}, u32[]{:S(2)}) collective-permute-start(bf16[1,6,3,10,256]{4,3,2,1,0:T(8,128)(2,1)S(1)} %get-tuple-element.23), channel_id=1, source_target_pairs={{0,8},{8,16},{16,24},{24,32},{32,40},{40,48},{48,56},{56,64},{64,7... | collective-permute-start | bytes 276488 | tf_op jit(solution)/shard_map/ppermute | solution.py:14
  44.4 9.7 %collective-permute-start.5 = (bf16[1,6,3,10,256]{4,3,2,1,0:T(8,128)(2,1)S(1)}, bf16[1,6,3,10,256]{4,3,2,1,0:T(8,128)(2,1)S(1)}, u32[]{:S(2)}, u32[]{:S(2)}) collective-permute-start(bf16[1,6,3,10,256]{4,3,2,1,0:T(8,128)(2,1)S(1)} %get-tuple-element.24), channel_id=1, source_target_pairs={{8,0},{16,8},{24,16},{32,24},{40,32},{48,40},{56,48},{64,56},{72,6... | collective-permute-start | bytes 276488 | tf_op jit(solution)/shard_map/ppermute | solution.py:17
  54.2 10.5 %collective-permute-start.6 = (bf16[8,1,3,10,256]{4,3,2,1,0:T(8,128)(2,1)S(1)}, bf16[8,1,3,10,256]{4,3,2,1,0:T(8,128)(2,1)S(1)}, u32[]{:S(2)}, u32[]{:S(2)}) collective-permute-start(bf16[8,1,3,10,256]{4,3,2,1,0:T(8,128)(2,1)S(1)} %get-tuple-element.19), channel_id=1, source_target_pairs={{0,1},{1,2},{2,3},{3,4},{4,5},{5,6},{6,7},{8,9},{9,10},{10,11},{11... | collective-permute-start | bytes 368648 | tf_op jit(solution)/shard_map/ppermute | solution.py:14
  59.3 9.1 %collective-permute-start.7 = (bf16[8,1,3,10,256]{4,3,2,1,0:T(8,128)(2,1)S(1)}, bf16[8,1,3,10,256]{4,3,2,1,0:T(8,128)(2,1)S(1)}, u32[]{:S(2)}, u32[]{:S(2)}) collective-permute-start(bf16[8,1,3,10,256]{4,3,2,1,0:T(8,128)(2,1)S(1)} %get-tuple-element.20), channel_id=1, source_target_pairs={{1,0},{2,1},{3,2},{4,3},{5,4},{6,5},{7,6},{9,8},{10,9},{11,10},{12... | collective-permute-start | bytes 368648 | tf_op jit(solution)/shard_map/ppermute | solution.py:17
  69.9 3.2 copy-start.7
  75.7 15.7 %all-to-all-start = ((bf16[8,128,256]{2,1,0:T(8,128)(2,1)}), bf16[8,128,256]{2,1,0:T(8,128)(2,1)S(1)}, u32[]{:S(2)}, u32[]{:S(2)}) async-start(bf16[8,128,256]{2,1,0:T(8,128)(2,1)} %stack.4), calls=%async_computation | async-start | bytes 1048576 | tf_op jit(solution)/shard_map/all_to_all | solution.py:61
  279.1 28.8 %copy-start.1 = (f32[6,6,3,10,256]{4,3,2,1,0:T(8,128)}, f32[6,6,3,10,256]{4,3,2,1,0:T(8,128)S(1)}, u32[]{:S(2)}) copy-start(f32[6,6,3,10,256]{4,3,2,1,0:T(8,128)S(1)} %slice_add_fusion.3) | copy-start | bytes 3317764
  279.2 7.2 %collective-permute-start.8 = (f32[1,6,3,10,256]{4,3,2,1,0:T(8,128)S(1)}, f32[1,6,3,10,256]{4,3,2,1,0:T(8,128)S(1)}, u32[]{:S(2)}, u32[]{:S(2)}) collective-permute-start(f32[1,6,3,10,256]{4,3,2,1,0:T(8,128)S(1)} %get-tuple-element.14), channel_id=1, source_target_pairs={{8,0},{16,8},{24,16},{32,24},{40,32},{48,40},{56,48},{64,56},{72,6... | collective-permute-start | bytes 552968 | tf_op jit(solution)/shard_map/ppermute | solution.py:17
  281.1 12.6 %collective-permute-start.9 = (f32[1,6,3,10,256]{4,3,2,1,0:T(8,128)S(1)}, f32[1,6,3,10,256]{4,3,2,1,0:T(8,128)S(1)}, u32[]{:S(2)}, u32[]{:S(2)}) collective-permute-start(f32[1,6,3,10,256]{4,3,2,1,0:T(8,128)S(1)} %get-tuple-element.13), channel_id=1, source_target_pairs={{0,8},{8,16},{16,24},{24,32},{32,40},{40,48},{48,56},{56,64},{64,7... | collective-permute-start | bytes 552968 | tf_op jit(solution)/shard_map/ppermute | solution.py:14
  293.8 11.2 %collective-permute-start.10 = (f32[8,1,3,10,256]{4,3,2,1,0:T(8,128)S(1)}, f32[8,1,3,10,256]{4,3,2,1,0:T(8,128)S(1)}, u32[]{:S(2)}, u32[]{:S(2)}) collective-permute-start(f32[8,1,3,10,256]{4,3,2,1,0:T(8,128)S(1)} %get-tuple-element.10), channel_id=1, source_target_pairs={{1,0},{2,1},{3,2},{4,3},{5,4},{6,5},{7,6},{9,8},{10,9},{11,10},{12... | collective-permute-start | bytes 737288 | tf_op jit(solution)/shard_map/ppermute | solution.py:17
  295.1 12.9 %copy-start.9 = (f32[6,6,3,10,256]{4,2,3,1,0:T(4,128)S(1)}, f32[6,6,3,10,256]{4,2,3,1,0:T(4,128)}, u32[]{:S(2)}) copy-start(f32[6,6,3,10,256]{4,2,3,1,0:T(4,128)} %param.7) | copy-start | bytes 3317764
  295.1 12.1 %collective-permute-start.11 = (f32[8,1,3,10,256]{4,3,2,1,0:T(8,128)S(1)}, f32[8,1,3,10,256]{4,3,2,1,0:T(8,128)S(1)}, u32[]{:S(2)}, u32[]{:S(2)}) collective-permute-start(f32[8,1,3,10,256]{4,3,2,1,0:T(8,128)S(1)} %get-tuple-element.9), channel_id=1, source_target_pairs={{0,1},{1,2},{2,3},{3,4},{4,5},{5,6},{6,7},{8,9},{9,10},{10,11},{11... | collective-permute-start | bytes 737288 | tf_op jit(solution)/shard_map/ppermute | solution.py:14
  309.3 8.6 %collective-permute-start.12 = (bf16[1,6,3,10,256]{4,3,2,1,0:T(8,128)(2,1)S(1)}, bf16[1,6,3,10,256]{4,3,2,1,0:T(8,128)(2,1)S(1)}, u32[]{:S(2)}, u32[]{:S(2)}) collective-permute-start(bf16[1,6,3,10,256]{4,3,2,1,0:T(8,128)(2,1)S(1)} %get-tuple-element.21), channel_id=1, source_target_pairs={{0,8},{8,16},{16,24},{24,32},{32,40},{40,48},{48,56},{56,64},{64,7... | collective-permute-start | bytes 276488 | tf_op jit(solution)/shard_map/ppermute | solution.py:14
  311.2 8.4 %collective-permute-start.13 = (bf16[1,6,3,10,256]{4,3,2,1,0:T(8,128)(2,1)S(1)}, bf16[1,6,3,10,256]{4,3,2,1,0:T(8,128)(2,1)S(1)}, u32[]{:S(2)}, u32[]{:S(2)}) collective-permute-start(bf16[1,6,3,10,256]{4,3,2,1,0:T(8,128)(2,1)S(1)} %get-tuple-element.22), channel_id=1, source_target_pairs={{8,0},{16,8},{24,16},{32,24},{40,32},{48,40},{56,48},{64,56},{72,6... | collective-permute-start | bytes 276488 | tf_op jit(solution)/shard_map/ppermute | solution.py:17
  319.7 9.2 %collective-permute-start.14 = (bf16[8,1,3,10,256]{4,3,2,1,0:T(8,128)(2,1)S(1)}, bf16[8,1,3,10,256]{4,3,2,1,0:T(8,128)(2,1)S(1)}, u32[]{:S(2)}, u32[]{:S(2)}) collective-permute-start(bf16[8,1,3,10,256]{4,3,2,1,0:T(8,128)(2,1)S(1)} %get-tuple-element.17), channel_id=1, source_target_pairs={{0,1},{1,2},{2,3},{3,4},{4,5},{5,6},{6,7},{8,9},{9,10},{10,11},{11... | collective-permute-start | bytes 368648 | tf_op jit(solution)/shard_map/ppermute | solution.py:14
  325.6 9.1 %collective-permute-start.15 = (bf16[8,1,3,10,256]{4,3,2,1,0:T(8,128)(2,1)S(1)}, bf16[8,1,3,10,256]{4,3,2,1,0:T(8,128)(2,1)S(1)}, u32[]{:S(2)}, u32[]{:S(2)}) collective-permute-start(bf16[8,1,3,10,256]{4,3,2,1,0:T(8,128)(2,1)S(1)} %get-tuple-element.18), channel_id=1, source_target_pairs={{1,0},{2,1},{3,2},{4,3},{5,4},{6,5},{7,6},{9,8},{10,9},{11,10},{12... | collective-permute-start | bytes 368648 | tf_op jit(solution)/shard_map/ppermute | solution.py:17
